TPU v7x, 128 devices: a whole 4x4x4 slice. The times are simulated.
128 devices in a mesh: replica: 8 (over z_hi, y), tensor: 16 (over x, z_lo, core).
Axes of the slice: x: 4, y: 4, z: 4 (z_hi: 2, z_lo: 2; z = z_hi * 2 + z_lo), core: 2. Of those that a mesh axis runs over, the one named last changes fastest.
Arguments:
- queries: bfloat16 [1024, 8192], P('replica', 'tensor'), may hold values from -200 to 200
- new_kv: bfloat16 [1024, 1024], P('replica'), may hold values from -8 to 8
- kv_pool: bfloat16 [1024, 64, 1024], P(('replica', 'tensor')), may hold values from -6 to 6
- anchor: int32 [8, 8], replicated, may hold values from 0 to 7, as said below
- page_table: int32 [64, 16], replicated, may hold values from 0 to 7, as said below
- prefix_len: int32 [64], replicated, may hold values from 1 to 1024, 32768 in all
- turn_rows: int32 [8, 8], replicated, may hold values from 1 to 32, 128 in all within a row
- out_weight: bfloat16 [8192, 16384], P('tensor', 'replica'), may hold values from -0.5 to 0.5
- residual: bfloat16 [1024, 16384], P(None, 'replica'), may hold values from -400 to 400
- norm_gain: bfloat16 [16384], P('replica'), may hold values from 0.099609375 to 1.8984375
- gate_up: bfloat16 [16384, 2, 26624], P('replica', None, 'tensor'), may hold values from -0.046875 to 0.046875
Outputs:
- hidden: bfloat16 [1024, 26624], P('replica', 'tensor')
Inputs may be any that keep to these rules, and one draw needn't show every extreme that they name: Slot j of new replica d holds session anchor[d, j] of old replica j; for each old replica, the 8 slots that come from it name each of its 8 sessions exactly once. `page_table`: row o * 8 + s lists the pages of session s of old replica o: entry k is a local page index on device k of that replica's 16 tensor devices, whose pages are numbered (o * 16 + k) * 8 + index in kv_pool; on each device the 8 sessions use distinct pages. `prefix_len`: indexed by d * 8 + j for slot j of new replica d. `turn_rows`: each replica's entries sum to 128.
All inputs are finite; a program needn't handle non-finite values.
Results may differ from a plain program's by a relative error of at most 0.0064.
Values may be sent and summed in bfloat16 or wider, within the bound.
A program may use at most 128 MiB of HBM per device.

v0:
```python
import jax
import jax.numpy as jnp
import numpy as np
from jax import lax
from jax.sharding import PartitionSpec as P

D = 16384
HD = 128
HEADS = 64
KVH = 4
PAGE = 64
SHARE = 1
ROWS = 128
GROUP = 16
EPSILON = 1e-05


def per_device(
    queries,
    new_kv,
    kv_pool,
    anchor,
    page_table,
    prefix_len,
    turn_rows,
    out_weight,
    residual,
    norm_gain,
    gate_up,
):
    replicas = lax.axis_size("replica")
    tensors = lax.axis_size("tensor")
    replica_idx = lax.axis_index("replica")
    tensor_idx = lax.axis_index("tensor")
    sessions = SHARE * replicas
    heads_local = HEADS // tensors
    pair_width = 2 * HD
    cached_len = tensors * PAGE
    owner_head = np.arange(tensors) * heads_local // GROUP
    from_here = lax.dynamic_slice_in_dim(anchor, replica_idx * SHARE, SHARE, 1)
    table_rows = lax.dynamic_slice_in_dim(page_table, replica_idx * sessions, sessions, 0)
    my_column = lax.dynamic_slice_in_dim(table_rows, tensor_idx, 1, 1)[:, 0]
    page_index = jnp.take(my_column, from_here.reshape(-1), axis=0)
    chosen = jnp.take(kv_pool, page_index, axis=0).reshape(replicas, SHARE, PAGE, KVH, pair_width)
    half = PAGE // 2
    lanes_per_head = tensors // KVH
    outgoing = jnp.transpose(chosen.reshape(replicas, 2, half, KVH, pair_width), (0, 3, 1, 2, 4))
    outgoing = jnp.broadcast_to(
        outgoing[:, :, None], (replicas, KVH, lanes_per_head // 2, 2, half, pair_width)
    ).reshape(replicas * tensors, SHARE, half, pair_width)
    arrived = lax.all_to_all(
        outgoing, ("replica", "tensor"), split_axis=0, concat_axis=0, tiled=True
    )
    partner = lax.ppermute(arrived, "tensor", [(i, i ^ 1) for i in range(tensors)])
    arrived = jnp.concatenate([arrived, partner], axis=2)
    arrived = arrived.reshape(replicas, tensors, SHARE, PAGE, pair_width)
    prefix_blocks = jnp.transpose(arrived, (0, 2, 1, 3, 4)).reshape(
        sessions, cached_len, pair_width
    )
    kv_group = tensor_idx * heads_local // GROUP
    fresh_pair = lax.dynamic_slice_in_dim(new_kv, kv_group * pair_width, pair_width, 1)
    rows_here = queries.shape[0]
    slot_rows = ROWS // 4
    query_heads = queries.reshape(rows_here, heads_local, HD)
    counts = lax.dynamic_slice_in_dim(turn_rows, replica_idx, 1, 0)[0]
    bounds = jnp.cumsum(counts, dtype=jnp.int32)
    starts = bounds - counts
    row_ids = jnp.arange(rows_here, dtype=jnp.int32)
    row_slot = jnp.sum(
        (row_ids[:, None] >= bounds[None, :]).astype(jnp.int32), axis=1, dtype=jnp.int32
    )
    offsets = jnp.arange(slot_rows, dtype=jnp.int32)
    padded_index = jnp.minimum(starts[:, None] + offsets[None, :], rows_here - 1).reshape(-1)
    slot_queries = jnp.take(query_heads, padded_index, axis=0).reshape(
        sessions, slot_rows, heads_local, HD
    )
    slot_fresh = jnp.take(fresh_pair, padded_index, axis=0).reshape(sessions, slot_rows, pair_width)
    lengths = lax.dynamic_slice_in_dim(prefix_len, replica_idx * sessions, sessions, 0)
    key_ids = jnp.arange(cached_len, dtype=jnp.int32)
    key_pos = key_ids // PAGE * PAGE + (key_ids % PAGE + tensor_idx % 2 * half) % PAGE
    prefix_mask = (key_pos[None, :] < lengths[:, None])[:, None, :]
    fresh_mask = (offsets[None, None, :] <= offsets[None, :, None]) & (
        offsets[None, None, :] < counts[:, None, None]
    )
    score_scale = HD ** (-0.5)
    prefix_scores = (
        jnp.einsum(
            "smhd,skd->hsmk",
            slot_queries,
            prefix_blocks[:, :, :HD],
            preferred_element_type=jnp.float32,
        )
        * score_scale
    )
    fresh_scores = (
        jnp.einsum(
            "smhd,snd->hsmn",
            slot_queries,
            slot_fresh[:, :, :HD],
            preferred_element_type=jnp.float32,
        )
        * score_scale
    )
    prefix_scores = jnp.where(prefix_mask[None], prefix_scores, -jnp.inf)
    fresh_scores = jnp.where(fresh_mask[None], fresh_scores, -jnp.inf)
    row_peak = jnp.maximum(jnp.max(prefix_scores, axis=3), jnp.max(fresh_scores, axis=3))
    prefix_weights = jnp.exp(prefix_scores - row_peak[..., None])
    fresh_weights = jnp.exp(fresh_scores - row_peak[..., None])
    denominator = jnp.sum(prefix_weights, axis=3) + jnp.sum(fresh_weights, axis=3)
    mixed_values = jnp.einsum(
        "hsmk,skd->smhd",
        prefix_weights.astype(jnp.bfloat16),
        prefix_blocks[:, :, HD:],
        preferred_element_type=jnp.float32,
    )
    mixed_values = mixed_values + jnp.einsum(
        "hsmn,snd->smhd",
        fresh_weights.astype(jnp.bfloat16),
        slot_fresh[:, :, HD:],
        preferred_element_type=jnp.float32,
    )
    slot_attended = (mixed_values / jnp.transpose(denominator, (1, 2, 0))[..., None]).astype(
        jnp.bfloat16
    )
    slot_attended = slot_attended.reshape(sessions * slot_rows, heads_local * HD)
    back_index = row_slot * slot_rows + row_ids - jnp.take(starts, row_slot, axis=0)
    attended = jnp.take(slot_attended, back_index, axis=0)
    gathered = lax.all_to_all(
        jnp.broadcast_to(attended[None], (replicas,) + attended.shape),
        "replica",
        split_axis=0,
        concat_axis=0,
        tiled=True,
    ).reshape(replicas * rows_here, attended.shape[1])
    partial_out = jnp.dot(gathered, out_weight, preferred_element_type=jnp.float32)
    all_rows = partial_out.shape[0]
    width = partial_out.shape[1]
    part_rows = all_rows // tensors
    head_parts = lax.all_to_all(
        partial_out.astype(jnp.bfloat16).reshape(tensors, part_rows, width),
        "tensor",
        split_axis=0,
        concat_axis=0,
        tiled=True,
    )
    head_sum = jnp.sum(head_parts.astype(jnp.float32), axis=0)
    my_residual = lax.dynamic_slice_in_dim(residual, tensor_idx * part_rows, part_rows, 0)
    carried = my_residual.astype(jnp.float32) + head_sum
    gain_row = norm_gain.astype(jnp.float32)
    own_squares = jnp.sum(carried * carried, axis=1)
    squares = jnp.sum(
        lax.all_to_all(
            jnp.broadcast_to(own_squares[None], (replicas,) + own_squares.shape),
            "replica",
            split_axis=0,
            concat_axis=0,
            tiled=True,
        ),
        axis=0,
    )
    normed_part = (carried * lax.rsqrt(squares / D + EPSILON)[:, None] * gain_row[None, :]).astype(
        jnp.bfloat16
    )
    normed = lax.all_gather(normed_part, "tensor", axis=0, tiled=True)
    weights_local = gate_up.reshape(gate_up.shape[0], 2 * gate_up.shape[2])
    slab = jnp.dot(normed, weights_local, preferred_element_type=jnp.float32)
    slab_parts = lax.all_to_all(
        slab.astype(jnp.bfloat16).reshape(replicas, rows_here, slab.shape[1]),
        "replica",
        split_axis=0,
        concat_axis=0,
        tiled=True,
    )
    summed = jnp.sum(slab_parts.astype(jnp.float32), axis=0)
    ff_here = gate_up.shape[2]
    gate = summed[:, :ff_here]
    up = summed[:, ff_here:]
    return (jax.nn.silu(gate) * up).astype(jnp.bfloat16)


def solution(mesh):
    placed = (
        P("replica", "tensor"),
        P("replica", None),
        P(("replica", "tensor"), None, None),
        P(),
        P(),
        P(),
        P(),
        P("tensor", "replica"),
        P(None, "replica"),
        P("replica"),
        P("replica", None, "tensor"),
    )
    return jax.shard_map(
        per_device, mesh=mesh, in_specs=placed, out_specs=P("replica", "tensor"), check_vma=False
    )
```

profile of v0, /device:TPU:1, one launch (start us, length us, event | category | flops | bytes accessed | tf_op | source)
XLA Modules:
  0.0 329.1 jit_solution(6830536024076237477)
XLA Ops:
  9.0 2.8 gather_fusion.1
  11.8 1.9 gather.38
  14.4 1.6 broadcast_in_dim.111
  16.0 11.9 %all-to-all-start = ((bf16[128,1,32,256]{3,2,1,0:T(8,128)(2,1)}), bf16[128,1,32,256]{3,2,1,0:T(8,128)(2,1)}, u32[]{:S(2)}, u32[]{:S(2)}) async-start(bf16[128,1,32,256]{3,2,1,0:T(8,128)(2,1)} %bitcast.141), calls=%async_computation | async-start | bytes 4194304 | tf_op jit(solution)/shard_map/all_to_all | solution.py:51
  31.2 26.0 %all-to-all-done = bf16[128,1,32,256]{3,2,1,0:T(8,128)(2,1)} async-done(((bf16[128,1,32,256]{3,2,1,0:T(8,128)(2,1)}), bf16[128,1,32,256]{3,2,1,0:T(8,128)(2,1)}, u32[]{:S(2)}, u32[]{:S(2)}) %all-to-all-start) | async-done | bytes 2097184 | tf_op jit(solution)/shard_map/all_to_all | solution.py:51
  57.2 1.3 collective-permute-start
  58.7 1.2 gather_fusion.3
  61.0 5.0 %compare_and_fusion.1 = (pred[128]{0:T(512)(128)(4,1)S(1)}, s32[128]{0:T(128)S(1)}) fusion(s32[128]{0:T(128)S(1)} %convert_reduce_fusion.2, s32[]{:T(128)} %bitcast.12, s32[]{:T(128)} %bitcast.11, s32[]{:T(128)} %bitcast.10, s32[]{:T(128)} %bitcast.9, s32[]{:T(128)} %bitcast.8, s32[]{:T(128)} %bitcast.7, s32[]{:T(128)} %bitcast.6, s32[]{:T(128)} %bitcast.5), kind=kLoop, calls=%fused_computation.99 | loop fusion | flops 4224 | bytes 1184 | tf_op jit(solution)/shard_map/jit(_take)/and | solution.py:127
  67.1 2.7 pad_maximum_fusion
  71.1 1.1 fusion.1
  72.2 1.4 fusion.21
  74.9 20.1 %all_to_all.26 = bf16[8,128,512]{2,1,0:T(8,128)(2,1)S(1)} all-to-all(bf16[8,128,512]{2,1,0:T(8,128)(2,1)S(1)} %broadcast_in_dim.122), channel_id=1, replica_groups=mesh['replica'=8,'tensor'=16] {'replica'}, dimensions={0} | all-to-all | bytes 2097152 | tf_op jit(solution)/shard_map/all_to_all | solution.py:128
  95.0 4.3 %convolution_convert_fusion.1 = bf16[1024,2048]{1,0:T(8,128)(2,1)} fusion(bf16[1024,512]{1,0:T(8,128)(2,1)S(1)} %bitcast.147, bf16[512,2048]{1,0:T(8,128)(2,1)S(1)} %copy-done), kind=kOutput, calls=%fused_computation.13 | convolution fusion | flops 2149580800 | bytes 7340032 | tf_op jit(solution)/shard_map/dot_general | solution.py:135
  99.3 5.1 %all-to-all-start.2 = ((bf16[16,64,2048]{2,1,0:T(8,128)(2,1)}), bf16[16,64,2048]{2,1,0:T(8,128)(2,1)}, u32[]{:S(2)}, u32[]{:S(2)}) async-start(bf16[16,64,2048]{2,1,0:T(8,128)(2,1)} %bitcast.146), calls=%async_computation.2 | async-start | bytes 8388608 | tf_op jit(solution)/shard_map/all_to_all | solution.py:139
  104.3 52.6 %all-to-all-done.2 = bf16[16,64,2048]{2,1,0:T(8,128)(2,1)} async-done(((bf16[16,64,2048]{2,1,0:T(8,128)(2,1)}), bf16[16,64,2048]{2,1,0:T(8,128)(2,1)}, u32[]{:S(2)}, u32[]{:S(2)}) %all-to-all-start.2) | async-done | bytes 4194336 | tf_op jit(solution)/shard_map/all_to_all | solution.py:139
  157.0 3.0 convert_reduce_fusion.1
  160.0 1.1 multiply_reduce_fusion
  161.7 3.3 %all-to-all-start.3 = ((f32[8,1,64]{2,1,0:T(1,128)}), f32[8,1,64]{2,1,0:T(1,128)S(1)}, u32[]{:S(2)}, u32[]{:S(2)}) async-start(f32[8,1,64]{2,1,0:T(1,128)} %broadcast_in_dim.123), calls=%async_computation.3 | async-start | bytes 8192 | tf_op jit(solution)/shard_map/all_to_all | solution.py:152
  165.3 6.1 %all-to-all-done.3 = f32[8,1,64]{2,1,0:T(1,128)S(1)} async-done(((f32[8,1,64]{2,1,0:T(1,128)}), f32[8,1,64]{2,1,0:T(1,128)S(1)}, u32[]{:S(2)}, u32[]{:S(2)}) %all-to-all-start.3) | async-done | bytes 2080 | tf_op jit(solution)/shard_map/all_to_all | solution.py:152
  171.5 1.8 multiply_convert_fusion
  173.2 14.2 %copy.57 = bf16[256,8,2,1664]{3,1,2,0:T(8,128)(2,1)} copy(bf16[256,8,2,1664]{3,2,1,0:T(2,128)(2,1)} %bitcast.139) | data formatting | bytes 27262976
  187.5 27.6 %all-gather.2.cloned.1.call-done = bf16[1024,2048]{1,0:T(8,128)(2,1)} async-done(((bf16[64,2048]{1,0:T(8,128)(2,1)}), bf16[1024,2048]{1,0:T(8,128)(2,1)}) %all-gather.2.cloned.1.call-update) | async-done | bytes 4194320 | tf_op jit(solution)/shard_map/all_gather | solution.py:164
  215.1 19.7 %convolution_convert_fusion = bf16[1024,3328]{1,0:T(8,128)(2,1)S(1)} fusion(bf16[1024,2048]{1,0:T(8,128)(2,1)} %all-gather.2.cloned.1.call-done, bf16[2048,3328]{1,0:T(8,128)(2,1)} %bitcast.140), kind=kOutput, calls=%fused_computation.7 | convolution fusion | flops 13962051584 | bytes 24641536 | tf_op jit(solution)/shard_map/dot_general | solution.py:166
  234.8 85.5 %all_to_all.27 = bf16[8,128,3328]{2,1,0:T(8,128)(2,1)S(1)} all-to-all(bf16[8,128,3328]{2,1,0:T(8,128)(2,1)S(1)} %bitcast.142), channel_id=1, replica_groups=mesh['replica'=8,'tensor'=16] {'replica'}, dimensions={0} | all-to-all | bytes 13631488 | tf_op jit(solution)/shard_map/all_to_all | solution.py:167
  (63 shorter events, 14.0 us)
Async XLA Ops:
  6.5 88.4 %copy-start = (bf16[512,2048]{1,0:T(8,128)(2,1)S(1)}, bf16[512,2048]{1,0:T(8,128)(2,1)}, u32[]{:S(2)}) copy-start(bf16[512,2048]{1,0:T(8,128)(2,1)} %param.18) | copy-start | bytes 6291460
  14.4 44.2 %copy-start.4 = (s32[64]{0:T(128)S(1)}, s32[64]{0:T(128)}, u32[]{:S(2)}) copy-start(s32[64]{0:T(128)} %param.16) | copy-start | bytes 772
  14.4 44.3 %copy-start.2 = (bf16[128,512]{1,0:T(8,128)(2,1)S(1)}, bf16[128,512]{1,0:T(8,128)(2,1)}, u32[]{:S(2)}) copy-start(bf16[128,512]{1,0:T(8,128)(2,1)} %param.11) | copy-start | bytes 393220
  16.0 41.3 %all-to-all-start = ((bf16[128,1,32,256]{3,2,1,0:T(8,128)(2,1)}), bf16[128,1,32,256]{3,2,1,0:T(8,128)(2,1)}, u32[]{:S(2)}, u32[]{:S(2)}) async-start(bf16[128,1,32,256]{3,2,1,0:T(8,128)(2,1)} %bitcast.141), calls=%async_computation | async-start | bytes 4194304 | tf_op jit(solution)/shard_map/all_to_all | solution.py:51
  57.2 9.8 %collective-permute-start = (bf16[128,1,32,256]{3,2,1,0:T(8,128)(2,1)}, bf16[128,1,32,256]{3,2,1,0:T(8,128)(2,1)}, u32[]{:S(2)}, u32[]{:S(2)}) collective-permute-start(bf16[128,1,32,256]{3,2,1,0:T(8,128)(2,1)} %all-to-all-done), channel_id=1, source_target_pairs={{0,1},{1,0},{2,3},{3,2},{4,5},{5,4},{6,7},{7,6},{8,9},{9,8},{10,11... | collective-permute-start | bytes 6291464 | tf_op jit(solution)/shard_map/ppermute | solution.py:54
  99.3 57.7 %all-to-all-start.2 = ((bf16[16,64,2048]{2,1,0:T(8,128)(2,1)}), bf16[16,64,2048]{2,1,0:T(8,128)(2,1)}, u32[]{:S(2)}, u32[]{:S(2)}) async-start(bf16[16,64,2048]{2,1,0:T(8,128)(2,1)} %bitcast.146), calls=%async_computation.2 | async-start | bytes 8388608 | tf_op jit(solution)/shard_map/all_to_all | solution.py:139
  104.3 60.9 %copy-start.3 = (bf16[2048]{0:T(1024)(128)(2,1)S(1)}, bf16[2048]{0:T(1024)(128)(2,1)}, u32[]{:S(2)}) copy-start(bf16[2048]{0:T(1024)(128)(2,1)} %param.20) | copy-start | bytes 12292
  161.7 9.7 %all-to-all-start.3 = ((f32[8,1,64]{2,1,0:T(1,128)}), f32[8,1,64]{2,1,0:T(1,128)S(1)}, u32[]{:S(2)}, u32[]{:S(2)}) async-start(f32[8,1,64]{2,1,0:T(1,128)} %broadcast_in_dim.123), calls=%async_computation.3 | async-start | bytes 8192 | tf_op jit(solution)/shard_map/all_to_all | solution.py:152
  165.0 50.0 %all-gather.2.cloned.1.call-start = ((), (), s32[]{:S(2)}) async-start(), calls=%async_computation.5 | async-start | bytes 4456448 | tf_op jit(solution)/shard_map/all_gather | solution.py:164
  234.8 87.5 %copy-start.1 = (bf16[512,2048]{1,0:T(8,128)(2,1)S(1)}, bf16[512,2048]{1,0:T(8,128)(2,1)}, u32[]{:S(2)}) copy-start(bf16[512,2048]{1,0:T(8,128)(2,1)} %param.18) | copy-start | bytes 6291460
Sparse Core Ops, SparseCore 0:
  173.4 41.6 all-gather.1
where the time goes:
time: 330 us; the launch traced here: 329 us
  waiting for transfers between devices  112 us (34%)
  blocking collectives  106 us (32%)
  local copies, waits for them, and re-layouts  29.4 us (9%)
  matrix products  27.2 us (8%)
  starting transfers between devices  21.9 us (7%)
  other arithmetic  19 us (6%)
  between operations  13.7 us (4%)
    all_to_all x1, blocking collectives, per_device(): lax.all_to_all(slab.astype(jnp.bfloat16).reshape(replicas, rows_here, sla...  85.5 us
    all_to_all x1, waiting for transfers between devices, per_device(): lax.all_to_all(partial_out.astype(jnp.bfloat16).reshape(tensors, part_row...  52.6 us
    all_gather x1, waiting for transfers between devices, per_device(): normed = lax.all_gather(normed_part, 'tensor', axis=0, tiled=True)  27.6 us
    all_to_all x1, waiting for transfers between devices, per_device(): lax.all_to_all(outgoing, ('replica', 'tensor'), split_axis=0, concat_axis...  26 us
    all_to_all x1, blocking collectives, per_device(): lax.all_to_all(jnp.broadcast_to(attended[None], (replicas,) + attended.sh...  20.1 us
    dot_general x1, matrix products, per_device(): slab = jnp.dot(normed, weights_local, preferred_element_type=jnp.float32)  19.7 us
    unnamed x13, local copies, waits for them, and re-layouts  14.4 us
    all_to_all x1, starting transfers between devices, per_device(): lax.all_to_all(outgoing, ('replica', 'tensor'), split_axis=0, concat_axis...  11.9 us
  transfers between devices with their start and end apart: 5, of which 4 were waited for; matrix products, arithmetic and copies ran while one was open for 8% of the time, Pallas kernels for 0%

commit v1 on v0

--- a/solution.py
+++ b/solution.py
@@ -161,7 +161,9 @@
     normed_part = (carried * lax.rsqrt(squares / D + EPSILON)[:, None] * gain_row[None, :]).astype(
         jnp.bfloat16
     )
-    normed = lax.all_gather(normed_part, "tensor", axis=0, tiled=True)
+    normed = jnp.concatenate(
+        lax.all_to_all(jnp.stack([normed_part] * lax.axis_size("tensor")), "tensor", 0, 0), axis=0
+    )
     weights_local = gate_up.reshape(gate_up.shape[0], 2 * gate_up.shape[2])
     slab = jnp.dot(normed, weights_local, preferred_element_type=jnp.float32)
     slab_parts = lax.all_to_all(

time: 330 us -> 344 us (1.042)
  the two profiles are of different devices: /device:TPU:1 before, /device:TPU:36 now
where the time goes in v1:
time: 344 us; the launch traced here: 343 us
  waiting for transfers between devices  134 us (39%)
  blocking collectives  103 us (30%)
  local copies, waits for them, and re-layouts  31.9 us (9%)
  starting transfers between devices  27.6 us (8%)
  matrix products  27.2 us (8%)
  other arithmetic  18.2 us (5%)
    all_to_all x1, blocking collectives, per_device(): lax.all_to_all(slab.astype(jnp.bfloat16).reshape(replicas, rows_here, sla...  82.5 us
    all_to_all x1, waiting for transfers between devices, per_device(): lax.all_to_all(partial_out.astype(jnp.bfloat16).reshape(tensors, part_row...  57.9 us
    all_to_all x1, waiting for transfers between devices, per_device(): lax.all_to_all(jnp.stack([normed_part] * lax.axis_size('tensor')), 'tenso...  44.9 us
    all_to_all x1, waiting for transfers between devices, per_device(): lax.all_to_all(outgoing, ('replica', 'tensor'), split_axis=0, concat_axis...  23.9 us
    all_to_all x1, blocking collectives, per_device(): lax.all_to_all(jnp.broadcast_to(attended[None], (replicas,) + attended.sh...  20.8 us
    dot_general x1, matrix products, per_device(): slab = jnp.dot(normed, weights_local, preferred_element_type=jnp.float32)  19.7 us
    unnamed x13, local copies, waits for them, and re-layouts  14.4 us
    all_to_all x1, starting transfers between devices, per_device(): lax.all_to_all(outgoing, ('replica', 'tensor'), split_axis=0, concat_axis...  10.7 us
  transfers between devices with their start and end apart: 5, of which 4 were waited for; matrix products, arithmetic and copies ran while one was open for 8% of the time, Pallas kernels for 0%

profile of v1, /device:TPU:36, one launch (start us, length us, event | category | flops | bytes accessed | tf_op | source)
XLA Modules:
  0.0 342.6 jit_solution(5088800375408503374)
XLA Ops:
  2.5 2.8 gather_fusion.1
  5.3 1.9 gather.38
  7.9 1.6 broadcast_in_dim.111
  9.5 10.7 %all-to-all-start = ((bf16[128,1,32,256]{3,2,1,0:T(8,128)(2,1)}), bf16[128,1,32,256]{3,2,1,0:T(8,128)(2,1)}, u32[]{:S(2)}, u32[]{:S(2)}) async-start(bf16[128,1,32,256]{3,2,1,0:T(8,128)(2,1)} %bitcast.142), calls=%async_computation | async-start | bytes 4194304 | tf_op jit(solution)/shard_map/all_to_all | solution.py:51
  23.4 23.9 %all-to-all-done = bf16[128,1,32,256]{3,2,1,0:T(8,128)(2,1)} async-done(((bf16[128,1,32,256]{3,2,1,0:T(8,128)(2,1)}), bf16[128,1,32,256]{3,2,1,0:T(8,128)(2,1)}, u32[]{:S(2)}, u32[]{:S(2)}) %all-to-all-start) | async-done | bytes 2097184 | tf_op jit(solution)/shard_map/all_to_all | solution.py:51
  47.9 1.2 gather_fusion.3
  50.2 5.0 %compare_and_fusion.1 = (pred[128]{0:T(512)(128)(4,1)S(1)}, s32[128]{0:T(128)S(1)}) fusion(s32[128]{0:T(128)S(1)} %convert_reduce_fusion.2, s32[]{:T(128)} %bitcast.12, s32[]{:T(128)} %bitcast.11, s32[]{:T(128)} %bitcast.10, s32[]{:T(128)} %bitcast.9, s32[]{:T(128)} %bitcast.8, s32[]{:T(128)} %bitcast.7, s32[]{:T(128)} %bitcast.6, s32[]{:T(128)} %bitcast.5), kind=kLoop, calls=%fused_computation.99 | loop fusion | flops 4224 | bytes 1184 | tf_op jit(solution)/shard_map/jit(_take)/and | solution.py:127
  56.2 2.7 pad_maximum_fusion
  60.3 1.1 fusion.1
  61.4 1.4 fusion.21
  64.1 20.8 %all_to_all.31 = bf16[8,128,512]{2,1,0:T(8,128)(2,1)S(1)} all-to-all(bf16[8,128,512]{2,1,0:T(8,128)(2,1)S(1)} %broadcast_in_dim.122), channel_id=1, replica_groups=mesh['replica'=8,'tensor'=16] {'replica'}, dimensions={0} | all-to-all | bytes 2097152 | tf_op jit(solution)/shard_map/all_to_all | solution.py:128
  84.9 4.3 %convolution_convert_fusion.1 = bf16[1024,2048]{1,0:T(8,128)(2,1)} fusion(bf16[1024,512]{1,0:T(8,128)(2,1)S(1)} %bitcast.148, bf16[512,2048]{1,0:T(8,128)(2,1)S(1)} %copy-done), kind=kOutput, calls=%fused_computation.13 | convolution fusion | flops 2149580800 | bytes 7340032 | tf_op jit(solution)/shard_map/dot_general | solution.py:135
  89.2 7.2 %all-to-all-start.2 = ((bf16[16,64,2048]{2,1,0:T(8,128)(2,1)}), bf16[16,64,2048]{2,1,0:T(8,128)(2,1)}, u32[]{:S(2)}, u32[]{:S(2)}) async-start(bf16[16,64,2048]{2,1,0:T(8,128)(2,1)} %bitcast.147), calls=%async_computation.2 | async-start | bytes 8388608 | tf_op jit(solution)/shard_map/all_to_all | solution.py:139
  96.4 57.9 %all-to-all-done.2 = bf16[16,64,2048]{2,1,0:T(8,128)(2,1)} async-done(((bf16[16,64,2048]{2,1,0:T(8,128)(2,1)}), bf16[16,64,2048]{2,1,0:T(8,128)(2,1)}, u32[]{:S(2)}, u32[]{:S(2)}) %all-to-all-start.2) | async-done | bytes 4194336 | tf_op jit(solution)/shard_map/all_to_all | solution.py:139
  154.3 3.0 convert_reduce_fusion.1
  157.3 1.1 multiply_reduce_fusion
  159.0 3.5 %all-to-all-start.3 = ((f32[8,1,64]{2,1,0:T(1,128)}), f32[8,1,64]{2,1,0:T(1,128)S(1)}, u32[]{:S(2)}, u32[]{:S(2)}) async-start(f32[8,1,64]{2,1,0:T(1,128)} %broadcast_in_dim.123), calls=%async_computation.3 | async-start | bytes 8192 | tf_op jit(solution)/shard_map/all_to_all | solution.py:152
  162.6 7.3 %all-to-all-done.3 = f32[8,1,64]{2,1,0:T(1,128)S(1)} async-done(((f32[8,1,64]{2,1,0:T(1,128)}), f32[8,1,64]{2,1,0:T(1,128)S(1)}, u32[]{:S(2)}, u32[]{:S(2)}) %all-to-all-start.3) | async-done | bytes 2080 | tf_op jit(solution)/shard_map/all_to_all | solution.py:152
  171.0 2.5 stack.2
  173.5 5.7 %all-to-all-start.4 = ((bf16[16,64,2048]{2,1,0:T(8,128)(2,1)}), bf16[16,64,2048]{2,1,0:T(8,128)(2,1)}, u32[]{:S(2)}, u32[]{:S(2)}) async-start(bf16[16,64,2048]{2,1,0:T(8,128)(2,1)} %stack.2), calls=%async_computation.4 | async-start | bytes 8388608 | tf_op jit(solution)/shard_map/all_to_all | solution.py:165
  179.2 14.2 %copy.57 = bf16[256,8,2,1664]{3,1,2,0:T(8,128)(2,1)} copy(bf16[256,8,2,1664]{3,2,1,0:T(2,128)(2,1)} %bitcast.140) | data formatting | bytes 27262976
  193.5 44.9 %all-to-all-done.4 = bf16[16,64,2048]{2,1,0:T(8,128)(2,1)} async-done(((bf16[16,64,2048]{2,1,0:T(8,128)(2,1)}), bf16[16,64,2048]{2,1,0:T(8,128)(2,1)}, u32[]{:S(2)}, u32[]{:S(2)}) %all-to-all-start.4) | async-done | bytes 4194336 | tf_op jit(solution)/shard_map/all_to_all | solution.py:165
  238.4 19.7 %convolution_convert_fusion = bf16[1024,3328]{1,0:T(8,128)(2,1)S(1)} fusion(bf16[1024,2048]{1,0:T(8,128)(2,1)} %bitcast.42, bf16[2048,3328]{1,0:T(8,128)(2,1)} %bitcast.141), kind=kOutput, calls=%fused_computation.7 | convolution fusion | flops 13962051584 | bytes 24641536 | tf_op jit(solution)/shard_map/dot_general | solution.py:168
  258.1 82.5 %all_to_all.32 = bf16[8,128,3328]{2,1,0:T(8,128)(2,1)S(1)} all-to-all(bf16[8,128,3328]{2,1,0:T(8,128)(2,1)S(1)} %bitcast.143), channel_id=1, replica_groups=mesh['replica'=8,'tensor'=16] {'replica'}, dimensions={0} | all-to-all | bytes 13631488 | tf_op jit(solution)/shard_map/all_to_all | solution.py:169
  (63 shorter events, 15.3 us)
Async XLA Ops:
  0.0 84.9 %copy-start = (bf16[512,2048]{1,0:T(8,128)(2,1)S(1)}, bf16[512,2048]{1,0:T(8,128)(2,1)}, u32[]{:S(2)}) copy-start(bf16[512,2048]{1,0:T(8,128)(2,1)} %param.18) | copy-start | bytes 6291460
  7.9 39.9 %copy-start.4 = (s32[64]{0:T(128)S(1)}, s32[64]{0:T(128)}, u32[]{:S(2)}) copy-start(s32[64]{0:T(128)} %param.16) | copy-start | bytes 772
  7.9 40.0 %copy-start.2 = (bf16[128,512]{1,0:T(8,128)(2,1)S(1)}, bf16[128,512]{1,0:T(8,128)(2,1)}, u32[]{:S(2)}) copy-start(bf16[128,512]{1,0:T(8,128)(2,1)} %param.11) | copy-start | bytes 393220
  9.5 37.9 %all-to-all-start = ((bf16[128,1,32,256]{3,2,1,0:T(8,128)(2,1)}), bf16[128,1,32,256]{3,2,1,0:T(8,128)(2,1)}, u32[]{:S(2)}, u32[]{:S(2)}) async-start(bf16[128,1,32,256]{3,2,1,0:T(8,128)(2,1)} %bitcast.142), calls=%async_computation | async-start | bytes 4194304 | tf_op jit(solution)/shard_map/all_to_all | solution.py:51
  47.3 8.9 %collective-permute-start = (bf16[128,1,32,256]{3,2,1,0:T(8,128)(2,1)}, bf16[128,1,32,256]{3,2,1,0:T(8,128)(2,1)}, u32[]{:S(2)}, u32[]{:S(2)}) collective-permute-start(bf16[128,1,32,256]{3,2,1,0:T(8,128)(2,1)} %all-to-all-done), channel_id=1, source_target_pairs={{0,1},{1,0},{2,3},{3,2},{4,5},{5,4},{6,7},{7,6},{8,9},{9,8},{10,11... | collective-permute-start | bytes 6291464 | tf_op jit(solution)/shard_map/ppermute | solution.py:54
  89.2 65.1 %all-to-all-start.2 = ((bf16[16,64,2048]{2,1,0:T(8,128)(2,1)}), bf16[16,64,2048]{2,1,0:T(8,128)(2,1)}, u32[]{:S(2)}, u32[]{:S(2)}) async-start(bf16[16,64,2048]{2,1,0:T(8,128)(2,1)} %bitcast.147), calls=%async_computation.2 | async-start | bytes 8388608 | tf_op jit(solution)/shard_map/all_to_all | solution.py:139
  96.4 66.1 %copy-start.3 = (bf16[2048]{0:T(1024)(128)(2,1)S(1)}, bf16[2048]{0:T(1024)(128)(2,1)}, u32[]{:S(2)}) copy-start(bf16[2048]{0:T(1024)(128)(2,1)} %param.20) | copy-start | bytes 12292
  159.0 10.9 %all-to-all-start.3 = ((f32[8,1,64]{2,1,0:T(1,128)}), f32[8,1,64]{2,1,0:T(1,128)S(1)}, u32[]{:S(2)}, u32[]{:S(2)}) async-start(f32[8,1,64]{2,1,0:T(1,128)} %broadcast_in_dim.123), calls=%async_computation.3 | async-start | bytes 8192 | tf_op jit(solution)/shard_map/all_to_all | solution.py:152
  173.5 64.9 %all-to-all-start.4 = ((bf16[16,64,2048]{2,1,0:T(8,128)(2,1)}), bf16[16,64,2048]{2,1,0:T(8,128)(2,1)}, u32[]{:S(2)}, u32[]{:S(2)}) async-start(bf16[16,64,2048]{2,1,0:T(8,128)(2,1)} %stack.2), calls=%async_computation.4 | async-start | bytes 8388608 | tf_op jit(solution)/shard_map/all_to_all | solution.py:165
  258.1 84.5 %copy-start.1 = (bf16[512,2048]{1,0:T(8,128)(2,1)S(1)}, bf16[512,2048]{1,0:T(8,128)(2,1)}, u32[]{:S(2)}) copy-start(bf16[512,2048]{1,0:T(8,128)(2,1)} %param.18) | copy-start | bytes 6291460
